TPU v7x, 256 devices: a whole 4x4x8 slice. The times are simulated.
256 devices in a mesh: dp: 32 (over z, y_lo, core), tensor: 8 (over x, y_hi).
Axes of the slice: x: 4, y: 4 (y_hi: 2, y_lo: 2; y = y_hi * 2 + y_lo), z: 8, core: 2. Of those that a mesh axis runs over, the one named last changes fastest.
Arguments:
- projected: bfloat16 [3, 16384, 2560], P(None, 'dp', 'tensor'), may hold values from -40 to 40
- residue_counts: int32 [32], P('dp'), may hold values from 64 to 512, as said below
- migrate_plan: int32 [32], P('dp'), may hold values from 0 to 1, as said below
- out_weight: bfloat16 [2560, 2560], P('tensor', 'dp'), may hold values from -0.125 to 0.125
- out_cotangent: bfloat16 [64, 512, 2560], P('dp', None, 'tensor'), may hold values from -6 to 6
Outputs:
- layer_out: bfloat16 [64, 512, 2560], P('dp', None, 'tensor')
- grad_projected: bfloat16 [3, 16384, 2560], P(None, 'dp', 'tensor')
- grad_weight: float32 [2560, 2560], P('tensor', 'dp')
Inputs may be any that keep to these rules, and one draw needn't show every extreme that they name: `residue_counts`: some tile has all 512 positions real, and some has exactly 64. migrate_plan[o] = 1 exactly where the sum of residue_counts over the 1 tiles of o exceeds that of its partner (o + 16) % 32 by more than 128, else 0; so never both devices of a pair have 1.
All inputs are finite; a program needn't handle non-finite values.
Results may differ from a plain program's by a relative error of at most 0.02.
Values may be sent and summed in bfloat16 or wider, within the bound.
No kernel may reach another device: no remote copies, remote signals or barrier semaphores. Data moves between devices by JAX's collectives and lax.ppermute only.
A program may use at most 128 MiB of HBM per device.

v0:
```python
import jax
import jax.numpy as jnp
from jax import lax
from jax.sharding import PartitionSpec as P

HEAD_DIM = 64


def shifted(shard, axis, by):
    peers = lax.axis_size(axis)
    return lax.ppermute(shard, axis, [(i, (i + by) % peers) for i in range(peers)])


def attend(tile_qkv, count):
    length = tile_qkv.shape[1]
    columns = tile_qkv.shape[2]
    head_count = columns // HEAD_DIM
    queries = tile_qkv[0].reshape(length, head_count, HEAD_DIM)
    key_rows = tile_qkv[1].reshape(length, head_count, HEAD_DIM)
    values = tile_qkv[2].reshape(length, head_count, HEAD_DIM)
    scores = jnp.einsum(
        "qhd,khd->hqk", queries, key_rows, preferred_element_type=jnp.float32
    ) * HEAD_DIM ** (-0.5)
    position = lax.iota(jnp.int32, length)
    live_mask = position < count
    scores = jnp.where(live_mask[None, None, :], scores, -1000000000.0)
    row_max = jnp.max(scores, axis=2, keepdims=True)
    exponent = jnp.exp(scores - row_max)
    weights = (exponent / jnp.sum(exponent, axis=2, keepdims=True)).astype(jnp.bfloat16)
    context = jnp.einsum("hqk,khd->qhd", weights, values, preferred_element_type=jnp.float32)
    context = context * live_mask.astype(jnp.float32)[:, None, None]
    return context.reshape(length, columns)


def tile_grad(tile_qkv, count, tile_cot):
    _, pullback = jax.vjp(lambda operand: attend(operand, count), tile_qkv)
    return pullback(tile_cot.astype(jnp.float32))[0]


def shards(projected, residue_counts, migrate_plan, out_weight, out_cotangent):
    home_tiles = residue_counts.shape[0]
    length = projected.shape[1] // home_tiles
    columns = projected.shape[2]
    half_axis = lax.axis_size("dp") // 2
    home_qkv = projected.reshape(3, home_tiles, length, columns)
    sent_flag = migrate_plan[0]
    guest_meta = jnp.stack([residue_counts[home_tiles - 1] * sent_flag, sent_flag])
    guest_tile, guest_info = shifted((home_qkv[:, home_tiles - 1], guest_meta), "dp", half_axis)
    slot_qkv = jnp.concatenate([home_qkv, guest_tile[:, None]], axis=1)
    keep_last = residue_counts[home_tiles - 1] * (1 - sent_flag)
    live_counts = jnp.concatenate(
        [residue_counts[: home_tiles - 1], keep_last[None], guest_info[0:1]]
    ).astype(jnp.int32)
    context = jax.vmap(attend, in_axes=(1, 0))(slot_qkv, live_counts).astype(jnp.bfloat16)
    row_count = context.shape[0] * length
    flat_ctx = context.reshape(row_count, columns)
    whole_weight = lax.all_gather(out_weight, "dp", axis=1, tiled=True)
    partial_value = jnp.dot(flat_ctx, whole_weight, preferred_element_type=jnp.float32)
    summed = lax.psum_scatter(
        partial_value.astype(jnp.bfloat16), "tensor", scatter_dimension=1, tiled=True
    )
    layer_out = summed.reshape(home_tiles + 1, length, -1)
    full_cot = lax.all_gather(out_cotangent, "tensor", axis=2, tiled=True).reshape(row_count, -1)
    contract_cols = (((1,), (1,)), ((), ()))
    grad_context = lax.dot_general(
        full_cot, whole_weight, contract_cols, preferred_element_type=jnp.float32
    )
    grad_context = grad_context.astype(jnp.bfloat16).reshape(home_tiles + 1, length, columns)
    weight_term = lax.dot_general(
        flat_ctx, full_cot, (((0,), (0,)), ((), ())), preferred_element_type=jnp.float32
    )
    grad_weight = lax.psum_scatter(
        weight_term.astype(jnp.bfloat16), "dp", scatter_dimension=1, tiled=True
    ).astype(jnp.float32)
    slot_grads = jax.vmap(tile_grad, in_axes=(1, 0, 0), out_axes=1)(
        slot_qkv, live_counts, grad_context
    )
    returned = shifted(slot_grads[:, home_tiles], "dp", half_axis)
    last_grad = jnp.where(sent_flag > 0, returned, slot_grads[:, home_tiles - 1])
    home_grads = jnp.concatenate([slot_grads[:, : home_tiles - 1], last_grad[:, None]], axis=1)
    grad_projected = home_grads.reshape(3, home_tiles * length, columns)
    return (layer_out, grad_projected, grad_weight)


def solution(mesh):
    in_specs = (
        P(None, "dp", "tensor"),
        P("dp"),
        P("dp"),
        P("tensor", "dp"),
        P("dp", None, "tensor"),
    )
    out_specs = (P("dp", None, "tensor"), P(None, "dp", "tensor"), P("tensor", "dp"))
    return jax.shard_map(shards, mesh=mesh, in_specs=in_specs, out_specs=out_specs, check_vma=False)
```

profile of v0, /device:TPU:1, one launch (start us, length us, event | category | flops | bytes accessed | tf_op | source)
XLA Modules:
  0.0 443.2 jit_solution(11317257145265913839)
XLA Ops:
  7.2 0.7 all-gather.5.cloned.1.call-update
  7.9 0.7 all-gather.3.cloned.1.call-update
  8.7 7.8 %collective-permute-start = (bf16[3,512,320]{1,2,0:T(8,128)(2,1)}, bf16[3,512,320]{1,2,0:T(8,128)(2,1)S(1)}, u32[]{:S(2)}, u32[]{:S(2)}) collective-permute-start(bf16[3,512,320]{1,2,0:T(8,128)(2,1)} %param.5), channel_id=1, source_target_pairs={{0,128},{8,136},{16,144},{24,152},{32,160},{40,168},{48,176},{56,1... | collective-permute-start | bytes 2949128 | tf_op jit(solution)/shard_map/ppermute | solution.py:11
  17.9 24.5 %collective-permute-done.1 = s32[2]{0:T(128)S(1)} collective-permute-done((s32[2]{0:T(128)S(1)}, s32[2]{0:T(128)S(1)}, u32[]{:S(2)}, u32[]{:S(2)}) %collective-permute-start.1) | collective-permute-done | bytes 40 | tf_op jit(solution)/shard_map/ppermute | solution.py:11
  42.6 1.3 pad_maximum_fusion
  44.0 2.5 fusion.5
  46.5 2.4 fusion.17
  49.0 1.6 copy-done
  50.6 48.2 %all-gather.5.cloned.1.call-done = bf16[2,512,2560]{1,2,0:T(8,128)(2,1)} async-done(((bf16[2,512,320]{1,2,0:T(8,128)(2,1)}), bf16[2,512,2560]{1,2,0:T(8,128)(2,1)}) %all-gather.5.cloned.1.call-update) | async-done | bytes 5242896 | tf_op jit(solution)/shard_map/all_gather | solution.py:63
  98.7 8.0 %copy.19 = bf16[2,512,2560]{2,1,0:T(8,128)(2,1)} copy(bf16[2,512,2560]{1,2,0:T(8,128)(2,1)} %all-gather.5.cloned.1.call-done) | data formatting | bytes 10485760 | tf_op jit(solution)/shard_map/all_gather | solution.py:63
  106.7 57.2 %all-gather.3.cloned.1.call-done = bf16[320,2560]{0,1:T(8,128)(2,1)} async-done(((bf16[320,80]{0,1:T(8,128)(2,1)}), bf16[320,2560]{0,1:T(8,128)(2,1)}) %all-gather.3.cloned.1.call-update) | async-done | bytes 1638416 | tf_op jit(solution)/shard_map/all_gather | solution.py:57
  163.9 6.1 %fusion.21 = f32[1024,320]{0,1:T(8,128)} fusion(bf16[1024,2560]{1,0:T(8,128)(2,1)} %bitcast.84, bf16[320,2560]{0,1:T(8,128)(2,1)} %all-gather.3.cloned.1.call-done), kind=kOutput, calls=%fused_computation.39 | convolution fusion | flops 1678376960 | bytes 8192000 | tf_op jit(solution)/shard_map/dot_general | solution.py:65
  170.1 2.5 reshape.93
  172.6 10.9 %convert_reduce_fusion = (f32[2,5,512]{2,1,0:T(8,128)S(1)}, pred[2,5,512,512]{2,3,1,0:T(32,128)(4,1)}, f32[2,5,512]{2,1,0:T(8,128)S(1)}, bf16[2,5,512,512]{2,3,1,0:T(8,128)(2,1)S(1)}) fusion(f32[2,5,512]{2,1,0:T(8,128)S(1)} %get-tuple-element.20, f32[2,5,512,512]{2,3,1,0:T(8,128)} %copy-done, pred[2,512]{1,0:T(4,128)(4,1)S(1)} %get-tuple-element.19, ...), kind=kOutput, calls=%fused_computation.7 | convolution fusion | flops 364697600 | bytes 20403200 | tf_op jit(solution)/shard_map/vmap(transpose(jvp(hqk,khd->qhd)))/dot_general | solution.py:30
  183.6 6.4 %fusion.34 = (f32[2,5,512]{2,1,0:T(8,128)S(1)}, f32[2,5,512,512]{2,3,1,0:T(8,128)}, bf16[2,5,512,512]{2,3,1,0:T(8,128)(2,1)S(1)}) fusion(f32[2,5,512]{2,1,0:T(8,128)S(1)} %get-tuple-element.20, f32[2,5,512,512]{2,3,1,0:T(8,128)S(1)} %bitcast.79, pred[2,512]{1,0:T(4,128)(4,1)S(1)} %get-tuple-element.19, f32[2,5,512]{2,1,0:T(8,128)S(1)} %neg.9, ...), kind=kLoop, calls=%fused_computation.62 | loop fusion | flops 26209280 | bytes 31540224 | tf_op jit(solution)/shard_map/vmap(transpose(jvp()))/reduce_sum | solution.py:28
  189.9 2.3 copy-done.1
  192.2 1.0 fusion.18
  193.2 4.3 fusion.16
  197.5 0.7 copy.18
  198.3 6.2 %convolution_convert_fusion = bf16[1024,2560]{0,1:T(8,128)(2,1)} fusion(bf16[320,2560]{0,1:T(8,128)(2,1)} %all-gather.3.cloned.1.call-done, bf16[1024,320]{0,1:T(8,128)(2,1)S(1)} %bitcast.99), kind=kOutput, calls=%fused_computation.15 | convolution fusion | flops 1680343040 | bytes 7536640 | tf_op jit(solution)/shard_map/dot_general | solution.py:58
  204.5 4.3 convolution_convert_fusion.2
  208.9 7.2 %fusion.20 = bf16[2,5,512,64]{2,3,1,0:T(8,128)(2,1)} fusion(bf16[2,512,5,64]{1,3,2,0:T(8,128)(2,1)S(1)} %bitcast.93, f32[2,5,512,512]{2,3,1,0:T(8,128)} %get-tuple-element.10, pred[2,5,512,512]{2,3,1,0:T(32,128)(4,1)} %get-tuple-element.12, f32[2,5,512]{2,1,0:T(8,128)S(1)} %negate_divide_fusion, pred[2,512]{1,0:T(4,128)(4,1)S(1)} %get-tuple-element.19), kind=kOutput, calls=%fused_computation.36 | convolution fusion | flops 346357760 | bytes 14439424 | tf_op jit(solution)/shard_map/vmap(transpose(jvp(qhd,khd->hqk)))/dot_general | solution.py:21
  216.1 4.6 %fusion.19 = bf16[2,5,512,64]{2,3,1,0:T(8,128)(2,1)S(1)} fusion(bf16[2,512,5,64]{1,3,2,0:T(8,128)(2,1)S(1)} %bitcast.91, f32[2,5,512,512]{2,3,1,0:T(8,128)S(1)} %bitcast.81, pred[2,5,512,512]{2,3,1,0:T(32,128)(4,1)} %get-tuple-element.12, f32[2,5,512]{2,1,0:T(8,128)S(1)} %negate_divide_fusion, pred[2,512]{1,0:T(4,128)(4,1)S(1)} %get-tuple-element.19), kind=kOutput, calls=%fused_computation.35 | convolution fusion | flops 346357760 | bytes 14439424 | tf_op jit(solution)/shard_map/vmap(transpose(jvp(qhd,khd->hqk)))/dot_general | solution.py:21
  220.7 0.2 add_bitcast_fusion
  220.9 1.0 slice_bitcast_fusion.1
  221.9 3.9 collective-permute-start.2
  225.7 43.2 %collective-permute-done.2 = bf16[3,512,320]{1,2,0:T(8,128)(2,1)S(1)} collective-permute-done((bf16[3,512,320]{1,2,0:T(8,128)(2,1)}, bf16[3,512,320]{1,2,0:T(8,128)(2,1)S(1)}, u32[]{:S(2)}, u32[]{:S(2)}) %collective-permute-start.2) | collective-permute-done | bytes 983072 | tf_op jit(solution)/shard_map/ppermute | solution.py:11
  269.0 1.0 fusion.24
  270.0 58.0 %reduce-scatter.5.cloned.1.call-done = bf16[320,80]{0,1:T(8,128)(2,1)} async-done(((bf16[320,2560]{0,1:T(8,128)(2,1)}), bf16[320,80]{0,1:T(8,128)(2,1)}) %reduce-scatter.5.cloned.1.call-update) | async-done | bytes 51216 | tf_op jit(solution)/shard_map/reduce_scatter | solution.py:72
  328.0 1.5 convert_element_type.92
  329.5 105.2 %reduce-scatter.3.cloned.1.call-done = bf16[1024,320]{0,1:T(8,128)(2,1)} async-done(((bf16[1024,2560]{0,1:T(8,128)(2,1)}), bf16[1024,320]{0,1:T(8,128)(2,1)}) %reduce-scatter.3.cloned.1.call-update) | async-done | bytes 655376 | tf_op jit(solution)/shard_map/reduce_scatter | solution.py:59
  434.7 2.0 copy.44
  (50 shorter events, 0.7 us)
Async XLA Ops:
  7.2 91.6 %all-gather.5.cloned.1.call-start = ((), (), s32[]{:S(2)}) async-start(), calls=%async_computation.4 | async-start | bytes 5898240 | tf_op jit(solution)/shard_map/all_gather | solution.py:63
  7.9 156.0 %all-gather.3.cloned.1.call-start = ((), (), s32[]{:S(2)}) async-start(), calls=%async_computation.2 | async-start | bytes 2027520 | tf_op jit(solution)/shard_map/all_gather | solution.py:57
  8.6 319.3 %reduce-scatter.5.cloned.1.call-start = ((), (), s32[]{:S(2)}) async-start(), calls=%async_computation.5 | async-start | bytes 2027520 | tf_op jit(solution)/shard_map/reduce_scatter | solution.py:72
  8.7 33.9 %collective-permute-start = (bf16[3,512,320]{1,2,0:T(8,128)(2,1)}, bf16[3,512,320]{1,2,0:T(8,128)(2,1)S(1)}, u32[]{:S(2)}, u32[]{:S(2)}) collective-permute-start(bf16[3,512,320]{1,2,0:T(8,128)(2,1)} %param.5), channel_id=1, source_target_pairs={{0,128},{8,136},{16,144},{24,152},{32,160},{40,168},{48,176},{56,1... | collective-permute-start | bytes 2949128 | tf_op jit(solution)/shard_map/ppermute | solution.py:11
  17.9 24.5 %collective-permute-start.1 = (s32[2]{0:T(128)S(1)}, s32[2]{0:T(128)S(1)}, u32[]{:S(2)}, u32[]{:S(2)}) collective-permute-start(s32[2]{0:T(128)S(1)} %pad_add_fusion), channel_id=1, source_target_pairs={{0,128},{8,136},{16,144},{24,152},{32,160},{40,168},{48,176},{56,1... | collective-permute-start | bytes 32 | tf_op jit(solution)/shard_map/ppermute | solution.py:11
  43.9 2.6 copy-start.4
  43.9 2.6 copy-start.6
  43.9 128.6 %copy-start.2 = (bf16[1,2,512,320]{2,3,0,1:T(8,128)(2,1)}, bf16[1,2,512,320]{2,3,0,1:T(8,128)(2,1)S(1)}, u32[]{:S(2)}) copy-start(bf16[1,2,512,320]{2,3,0,1:T(8,128)(2,1)S(1)} %get-tuple-element.16) | copy-start | bytes 1966084
  46.5 4.0 copy-start
  170.0 23.1 %slice-start.6 = ((s8[5242880]{0:T(1024)(128)(4,1)}), s8[1048576]{0:T(1024)(128)(4,1)S(1)}, s32[]{:S(2)}) async-start(s8[5242880]{0:T(1024)(128)(4,1)} %bitcast.82), calls=%async_computation.12 | async-start | bytes 2097152
  172.5 11.0 %slice-start = ((s8[10485760]{0:T(1024)(128)(4,1)}), s8[4194304]{0:T(1024)(128)(4,1)S(1)}, s32[]{:S(2)}) async-start(s8[10485760]{0:T(1024)(128)(4,1)} %bitcast.78), calls=%async_computation.6 | async-start | bytes 8388608
  172.6 11.0 %slice-start.1 = ((s8[10485760]{0:T(1024)(128)(4,1)}), s8[4194304]{0:T(1024)(128)(4,1)S(1)}, s32[]{:S(2)}) async-start(s8[10485760]{0:T(1024)(128)(4,1)} %bitcast.78), calls=%async_computation.7 | async-start | bytes 8388608
  172.6 11.0 %slice-start.2 = ((s8[10485760]{0:T(1024)(128)(4,1)}), s8[2097152]{0:T(1024)(128)(4,1)S(1)}, s32[]{:S(2)}) async-start(s8[10485760]{0:T(1024)(128)(4,1)} %bitcast.78), calls=%async_computation.8 | async-start | bytes 4194304
  172.6 20.6 %slice-start.7 = ((s8[5242880]{0:T(1024)(128)(4,1)}), s8[4194304]{0:T(1024)(128)(4,1)S(1)}, s32[]{:S(2)}) async-start(s8[5242880]{0:T(1024)(128)(4,1)} %bitcast.82), calls=%async_computation.13 | async-start | bytes 8388608
  183.6 8.6 %copy-start.3 = (bf16[1,2,512,320]{2,3,0,1:T(8,128)(2,1)S(1)}, bf16[1,2,512,320]{2,3,0,1:T(8,128)(2,1)}, u32[]{:S(2)}) copy-start(bf16[1,2,512,320]{2,3,0,1:T(8,128)(2,1)} %copy-done.2) | copy-start | bytes 1966084
  189.9 2.3 copy-start.1
  197.5 237.2 %reduce-scatter.3.cloned.1.call-start = ((), (), s32[]{:S(2)}) async-start(), calls=%async_computation.3 | async-start | bytes 5898240 | tf_op jit(solution)/shard_map/reduce_scatter | solution.py:59
  204.5 4.4 copy-start.7
  204.5 11.5 %slice-start.3 = ((s8[10485760]{0:T(1024)(128)(4,1)}), s8[4194304]{0:T(1024)(128)(4,1)S(1)}, s32[]{:S(2)}) async-start(s8[10485760]{0:T(1024)(128)(4,1)} %bitcast.80), calls=%async_computation.9 | async-start | bytes 8388608
  208.9 7.2 %slice-start.4 = ((s8[10485760]{0:T(1024)(128)(4,1)}), s8[4194304]{0:T(1024)(128)(4,1)S(1)}, s32[]{:S(2)}) async-start(s8[10485760]{0:T(1024)(128)(4,1)} %bitcast.80), calls=%async_computation.10 | async-start | bytes 8388608
  208.9 7.2 %slice-start.5 = ((s8[10485760]{0:T(1024)(128)(4,1)}), s8[2097152]{0:T(1024)(128)(4,1)S(1)}, s32[]{:S(2)}) async-start(s8[10485760]{0:T(1024)(128)(4,1)} %bitcast.80), calls=%async_computation.11 | async-start | bytes 4194304
  208.9 7.2 %copy-start.5 = (bf16[1,2,512,320]{2,3,0,1:T(8,128)(2,1)S(1)}, bf16[1,2,512,320]{2,3,0,1:T(8,128)(2,1)}, u32[]{:S(2)}) copy-start(bf16[1,2,512,320]{2,3,0,1:T(8,128)(2,1)} %copy-done.4) | copy-start | bytes 1966084
  216.1 4.6 %copy-start.8 = (bf16[2,5,512,64]{2,3,1,0:T(8,128)(2,1)S(1)}, bf16[2,5,512,64]{2,3,1,0:T(8,128)(2,1)}, u32[]{:S(2)}) copy-start(bf16[2,5,512,64]{2,3,1,0:T(8,128)(2,1)} %fusion.20) | copy-start | bytes 1966084
  221.9 47.1 %collective-permute-start.2 = (bf16[3,512,320]{1,2,0:T(8,128)(2,1)}, bf16[3,512,320]{1,2,0:T(8,128)(2,1)S(1)}, u32[]{:S(2)}, u32[]{:S(2)}) collective-permute-start(bf16[3,512,320]{1,2,0:T(8,128)(2,1)} %slice_bitcast_fusion.1), channel_id=1, source_target_pairs={{0,128},{8,136},{16,144},{24,152},{32,160},{40,168},{48,176},{56,1... | collective-permute-start | bytes 2949128 | tf_op jit(solution)/shard_map/ppermute | solution.py:11
Sparse Core Ops, SparseCore 0:
  10.6 88.1 all-gather.4
  100.6 63.3 all-gather.2
  197.6 130.3 reduce-scatter.4
  332.0 102.6 reduce-scatter.2
where the time goes:
time: 444 us; the launch traced here: 443 us
  waiting for transfers between devices  338 us (76%)
  matrix products  47 us (11%)
  local copies, waits for them, and re-layouts  18.1 us (4%)
  between operations  15.4 us (3%)
  other arithmetic  13.1 us (3%)
  starting transfers between devices  11.9 us (3%)
    reduce_scatter x1, waiting for transfers between devices, shards(): lax.psum_scatter(partial_value.astype(jnp.bfloat16), 'tensor', scatter_di...  105 us
    ppermute x3, waiting for transfers between devices, shifted(): lax.ppermute(shard, axis, [(i, (i + by) % peers) for i in range(peers)])  67.7 us
    reduce_scatter x1, waiting for transfers between devices, shards(): lax.psum_scatter(weight_term.astype(jnp.bfloat16), 'dp', scatter_dimensio...  58 us
    all_gather x1, waiting for transfers between devices, shards(): whole_weight = lax.all_gather(out_weight, 'dp', axis=1, tiled=True)  57.2 us
    all_gather x1, waiting for transfers between devices, shards(): lax.all_gather(out_cotangent, 'tensor', axis=2, tiled=True)  48.2 us
    dot_general x3, matrix products, attend(): jnp.einsum('hqk,khd->qhd', weights, values, preferred_element_type=jnp.fl...  16.2 us
    dot_general x3, matrix products, attend(): jnp.einsum('qhd,khd->hqk', queries, key_rows, preferred_element_type=jnp....  14.3 us
    ppermute x3, starting transfers between devices, shifted(): lax.ppermute(shard, axis, [(i, (i + by) % peers) for i in range(peers)])  11.7 us
  transfers between devices with their start and end apart: 7, of which 6 were waited for; matrix products, arithmetic and copies ran while one was open for 9% of the time, Pallas kernels for 0%

commit v1 on v0

--- a/solution.py
+++ b/solution.py
@@ -4,6 +4,13 @@
 from jax.sharding import PartitionSpec as P
 
 HEAD_DIM = 64
+
+
+def gather_over(array, axis, along):
+    n_dev = lax.axis_size(axis)
+    blocks = jnp.stack([array for _ in range(n_dev)])
+    blocks = lax.all_to_all(blocks, axis, split_axis=0, concat_axis=0)
+    return jnp.concatenate(blocks, axis=along)
 
 
 def shifted(shard, axis, by):
@@ -60,7 +67,7 @@
         partial_value.astype(jnp.bfloat16), "tensor", scatter_dimension=1, tiled=True
     )
     layer_out = summed.reshape(home_tiles + 1, length, -1)
-    full_cot = lax.all_gather(out_cotangent, "tensor", axis=2, tiled=True).reshape(row_count, -1)
+    full_cot = gather_over(out_cotangent, "tensor", 2).reshape(row_count, -1)
     contract_cols = (((1,), (1,)), ((), ()))
     grad_context = lax.dot_general(
         full_cot, whole_weight, contract_cols, preferred_element_type=jnp.float32

time: 444 us -> 403 us (0.908)
  waiting for transfers between devices: 338 us -> 286 us
  starting transfers between devices: 11.9 us -> 18.7 us
  local copies, waits for them, and re-layouts: 18.1 us -> 23.5 us
    all_gather x1 -> x0, waiting for transfers between devices: 48.2 us -> none  [shards(): lax.all_gather(out_cotangent, 'tensor', axis=2, tiled=True)]
    all_gather x1, waiting for transfers between devices: 57.2 us -> 18.6 us  [shards(): whole_weight = lax.all_gather(out_weight, 'dp', axis=1, tiled=True)]
    all_to_all x0 -> x1, waiting for transfers between devices: none -> 31.5 us  [gather_over(): blocks = lax.all_to_all(blocks, axis, split_axis=0, concat_axis=0)]
    reduce_scatter x1, waiting for transfers between devices: 58 us -> 69.1 us  [shards(): lax.psum_scatter(weight_term.astype(jnp.bfloat16), 'dp', scatter_dimensio...]
    unnamed x35, local copies, waits for them, and re-layouts: 3.98 us -> 12.3 us
    all_gather x1 -> x0, local copies, waits for them, and re-layouts: 7.98 us -> none  [shards(): lax.all_gather(out_cotangent, 'tensor', axis=2, tiled=True)]
    all_to_all x0 -> x1, starting transfers between devices: none -> 7.6 us  [gather_over(): blocks = lax.all_to_all(blocks, axis, split_axis=0, concat_axis=0)]
    reduce_scatter x1, waiting for transfers between devices: 105 us -> 98.9 us  [shards(): lax.psum_scatter(partial_value.astype(jnp.bfloat16), 'tensor', scatter_di...]
where the time goes in v1:
time: 403 us
  waiting for transfers between devices  286 us (71%)
  matrix products  46.8 us (12%)
  local copies, waits for them, and re-layouts  23.5 us (6%)
  starting transfers between devices  18.7 us (5%)
  between operations  15.3 us (4%)
  other arithmetic  12.2 us (3%)
    reduce_scatter x1, waiting for transfers between devices, shards(): lax.psum_scatter(partial_value.astype(jnp.bfloat16), 'tensor', scatter_di...  98.9 us
    reduce_scatter x1, waiting for transfers between devices, shards(): lax.psum_scatter(weight_term.astype(jnp.bfloat16), 'dp', scatter_dimensio...  69.1 us
    ppermute x3, waiting for transfers between devices, shifted(): lax.ppermute(shard, axis, [(i, (i + by) % peers) for i in range(peers)])  67.2 us
    all_to_all x1, waiting for transfers between devices, gather_over(): blocks = lax.all_to_all(blocks, axis, split_axis=0, concat_axis=0)  31.5 us
    all_gather x1, waiting for transfers between devices, shards(): whole_weight = lax.all_gather(out_weight, 'dp', axis=1, tiled=True)  18.6 us
    dot_general x3, matrix products, attend(): jnp.einsum('hqk,khd->qhd', weights, values, preferred_element_type=jnp.fl...  16.2 us
    dot_general x3, matrix products, attend(): jnp.einsum('qhd,khd->hqk', queries, key_rows, preferred_element_type=jnp....  14.3 us
    unnamed x35, local copies, waits for them, and re-layouts  12.3 us
  transfers between devices with their start and end apart: 7, of which 6 were waited for; matrix products, arithmetic and copies ran while one was open for 9% of the time, Pallas kernels for 0%

profile of v1, /device:TPU:1, one launch (start us, length us, event | category | flops | bytes accessed | tf_op | source)
XLA Modules:
  0.0 402.5 jit_solution(3315725192377750830)
XLA Ops:
  7.2 1.8 copy.20
  8.9 5.0 %stack.8 = bf16[8,2,512,320]{2,1,3,0:T(2,128)(2,1)} broadcast(bf16[2,512,320]{1,0,2:T(2,128)(2,1)S(1)} %copy.20), dimensions={1,2,3} | broadcast | bytes 5898240 | tf_op jit(solution)/shard_map/stack | solution.py:11
  14.0 7.6 %all-to-all-start = ((bf16[8,2,512,320]{2,1,3,0:T(2,128)(2,1)}), bf16[8,2,512,320]{2,1,3,0:T(2,128)(2,1)}, u32[]{:S(2)}, u32[]{:S(2)}) async-start(bf16[8,2,512,320]{2,1,3,0:T(2,128)(2,1)} %stack.8), calls=%async_computation.1 | async-start | bytes 10485760 | tf_op jit(solution)/shard_map/all_to_all | solution.py:12
  21.6 0.7 all-gather.2.cloned.1.call-update
  22.4 7.0 %collective-permute-start = (bf16[3,512,320]{1,2,0:T(8,128)(2,1)S(1)}, bf16[3,512,320]{1,2,0:T(8,128)(2,1)S(1)}, u32[]{:S(2)}, u32[]{:S(2)}) collective-permute-start(bf16[3,512,320]{1,2,0:T(8,128)(2,1)S(1)} %copy-done.6), channel_id=1, source_target_pairs={{0,128},{8,136},{16,144},{24,152},{32,160},{40,168},{48,176},{56,1... | collective-permute-start | bytes 2949128 | tf_op jit(solution)/shard_map/ppermute | solution.py:18
  31.0 25.2 %collective-permute-done.1 = s32[2]{0:T(128)S(1)} collective-permute-done((s32[2]{0:T(128)S(1)}, s32[2]{0:T(128)S(1)}, u32[]{:S(2)}, u32[]{:S(2)}) %collective-permute-start.1) | collective-permute-done | bytes 40 | tf_op jit(solution)/shard_map/ppermute | solution.py:18
  56.5 2.5 fusion.5
  59.1 2.4 fusion.16
  61.6 1.5 copy-done
  63.1 31.5 %all-to-all-done = bf16[8,2,512,320]{2,1,3,0:T(2,128)(2,1)} async-done(((bf16[8,2,512,320]{2,1,3,0:T(2,128)(2,1)}), bf16[8,2,512,320]{2,1,3,0:T(2,128)(2,1)}, u32[]{:S(2)}, u32[]{:S(2)}) %all-to-all-start) | async-done | bytes 5242912 | tf_op jit(solution)/shard_map/all_to_all | solution.py:12
  94.6 6.6 %copy.35 = bf16[320,8,2,512]{3,1,2,0:T(8,128)(2,1)} copy(bf16[320,8,2,512]{3,2,1,0:T(2,128)(2,1)} %bitcast.39) | data formatting | bytes 10485760
  101.2 18.6 %all-gather.2.cloned.1.call-done = bf16[320,2560]{0,1:T(8,128)(2,1)} async-done(((bf16[320,80]{0,1:T(8,128)(2,1)}), bf16[320,2560]{0,1:T(8,128)(2,1)}) %all-gather.2.cloned.1.call-update) | async-done | bytes 1638416 | tf_op jit(solution)/shard_map/all_gather | solution.py:64
  119.8 6.1 %fusion.20 = f32[1024,320]{0,1:T(8,128)} fusion(bf16[1024,2560]{0,1:T(8,128)(2,1)} %bitcast.82, bf16[320,2560]{0,1:T(8,128)(2,1)} %all-gather.2.cloned.1.call-done), kind=kOutput, calls=%fused_computation.38 | convolution fusion | flops 1678376960 | bytes 8192000 | tf_op jit(solution)/shard_map/dot_general | solution.py:72
  125.9 2.5 reshape.95
  128.4 10.9 %convert_reduce_fusion = (f32[2,5,512]{2,1,0:T(8,128)S(1)}, pred[2,5,512,512]{2,3,1,0:T(32,128)(4,1)}, f32[2,5,512]{2,1,0:T(8,128)S(1)}, bf16[2,5,512,512]{2,3,1,0:T(8,128)(2,1)S(1)}) fusion(f32[2,5,512]{2,1,0:T(8,128)S(1)} %get-tuple-element.20, f32[2,5,512,512]{2,3,1,0:T(8,128)} %copy-done, pred[2,512]{1,0:T(4,128)(4,1)S(1)} %get-tuple-element.19, ...), kind=kOutput, calls=%fused_computation.7 | convolution fusion | flops 364697600 | bytes 20403200 | tf_op jit(solution)/shard_map/vmap(transpose(jvp(hqk,khd->qhd)))/dot_general | solution.py:37
  139.3 6.6 %fusion.34 = (f32[2,5,512]{2,1,0:T(8,128)S(1)}, f32[2,5,512,512]{2,3,1,0:T(8,128)}, bf16[2,5,512,512]{2,3,1,0:T(8,128)(2,1)S(1)}) fusion(f32[2,5,512]{2,1,0:T(8,128)S(1)} %get-tuple-element.20, f32[2,5,512,512]{2,3,1,0:T(8,128)S(1)} %bitcast.79, pred[2,512]{1,0:T(4,128)(4,1)S(1)} %get-tuple-element.19, f32[2,5,512]{2,1,0:T(8,128)S(1)} %neg.9, ...), kind=kLoop, calls=%fused_computation.62 | loop fusion | flops 26209280 | bytes 31540224 | tf_op jit(solution)/shard_map/vmap(transpose(jvp()))/reduce_sum | solution.py:35
  145.9 2.2 copy-done.1
  148.1 1.0 fusion.23
  149.1 0.7 copy.19
  149.9 4.1 %convolution_convert_fusion.1 = bf16[320,2560]{0,1:T(8,128)(2,1)} fusion(bf16[1024,320]{0,1:T(8,128)(2,1)S(1)} %bitcast.97, bf16[1024,2560]{0,1:T(8,128)(2,1)S(1)} %bitcast.85), kind=kOutput, calls=%fused_computation.24 | convolution fusion | flops 1678540800 | bytes 7536640 | tf_op jit(solution)/shard_map/dot_general | solution.py:76
  154.1 6.1 %convolution_convert_fusion = bf16[1024,2560]{0,1:T(8,128)(2,1)} fusion(bf16[320,2560]{0,1:T(8,128)(2,1)} %all-gather.2.cloned.1.call-done, bf16[1024,320]{0,1:T(8,128)(2,1)S(1)} %bitcast.98), kind=kOutput, calls=%fused_computation.15 | convolution fusion | flops 1680343040 | bytes 7536640 | tf_op jit(solution)/shard_map/dot_general | solution.py:65
  160.3 4.3 %convolution_convert_fusion.3 = bf16[2,5,64,512]{3,2,1,0:T(8,128)(2,1)S(1)} fusion(bf16[2,5,512,512]{2,3,1,0:T(8,128)(2,1)} %copy-done.1, f32[2,512,5,64]{1,0,3,2:T(2,128)S(1)} %reshape.95, f32[2,512]{1,0:T(2,128)S(1)} %get-tuple-element.18), kind=kOutput, calls=%fused_computation.36 | convolution fusion | flops 336199680 | bytes 7213056 | tf_op jit(solution)/shard_map/vmap(transpose(jvp(hqk,khd->qhd)))/dot_general | solution.py:37
  164.7 7.2 %fusion.19 = bf16[2,5,512,64]{2,3,1,0:T(8,128)(2,1)} fusion(bf16[2,512,5,64]{1,3,2,0:T(8,128)(2,1)S(1)} %bitcast.92, f32[2,5,512,512]{2,3,1,0:T(8,128)} %get-tuple-element.10, pred[2,5,512,512]{2,3,1,0:T(32,128)(4,1)} %get-tuple-element.12, f32[2,5,512]{2,1,0:T(8,128)S(1)} %negate_divide_fusion, pred[2,512]{1,0:T(4,128)(4,1)S(1)} %get-tuple-element.19), kind=kOutput, calls=%fused_computation.35 | convolution fusion | flops 346357760 | bytes 14439424 | tf_op jit(solution)/shard_map/vmap(transpose(jvp(qhd,khd->hqk)))/dot_general | solution.py:28
  171.9 4.6 %fusion.18 = bf16[2,5,512,64]{2,3,1,0:T(8,128)(2,1)S(1)} fusion(bf16[2,512,5,64]{1,3,2,0:T(8,128)(2,1)S(1)} %bitcast.90, f32[2,5,512,512]{2,3,1,0:T(8,128)S(1)} %bitcast.81, pred[2,5,512,512]{2,3,1,0:T(32,128)(4,1)} %get-tuple-element.12, f32[2,5,512]{2,1,0:T(8,128)S(1)} %negate_divide_fusion, pred[2,512]{1,0:T(4,128)(4,1)S(1)} %get-tuple-element.19), kind=kOutput, calls=%fused_computation.34 | convolution fusion | flops 346357760 | bytes 14439424 | tf_op jit(solution)/shard_map/vmap(transpose(jvp(qhd,khd->hqk)))/dot_general | solution.py:28
  176.7 1.0 slice_bitcast_fusion.1
  177.7 3.8 collective-permute-start.2
  181.5 42.0 %collective-permute-done.2 = bf16[3,512,320]{1,2,0:T(8,128)(2,1)S(1)} collective-permute-done((bf16[3,512,320]{1,2,0:T(8,128)(2,1)}, bf16[3,512,320]{1,2,0:T(8,128)(2,1)S(1)}, u32[]{:S(2)}, u32[]{:S(2)}) %collective-permute-start.2) | collective-permute-done | bytes 983072 | tf_op jit(solution)/shard_map/ppermute | solution.py:18
  223.5 1.0 fusion.24
  224.5 69.1 %reduce-scatter.5.cloned.1.call-done = bf16[320,80]{0,1:T(8,128)(2,1)} async-done(((bf16[320,2560]{0,1:T(8,128)(2,1)}), bf16[320,80]{0,1:T(8,128)(2,1)}) %reduce-scatter.5.cloned.1.call-update) | async-done | bytes 51216 | tf_op jit(solution)/shard_map/reduce_scatter | solution.py:79
  293.6 1.5 convert_element_type.89
  295.1 98.9 %reduce-scatter.3.cloned.1.call-done = bf16[1024,320]{0,1:T(8,128)(2,1)} async-done(((bf16[1024,2560]{0,1:T(8,128)(2,1)}), bf16[1024,320]{0,1:T(8,128)(2,1)}) %reduce-scatter.3.cloned.1.call-update) | async-done | bytes 655376 | tf_op jit(solution)/shard_map/reduce_scatter | solution.py:66
  394.0 2.0 copy.46
  (49 shorter events, 1.2 us)
Async XLA Ops:
  14.0 8.4 %copy-start.6 = (bf16[3,512,320]{1,2,0:T(8,128)(2,1)S(1)}, bf16[3,512,320]{1,2,0:T(8,128)(2,1)}, u32[]{:S(2)}) copy-start(bf16[3,512,320]{1,2,0:T(8,128)(2,1)} %param.5) | copy-start | bytes 2949124
  14.0 80.6 %all-to-all-start = ((bf16[8,2,512,320]{2,1,3,0:T(2,128)(2,1)}), bf16[8,2,512,320]{2,1,3,0:T(2,128)(2,1)}, u32[]{:S(2)}, u32[]{:S(2)}) async-start(bf16[8,2,512,320]{2,1,3,0:T(2,128)(2,1)} %stack.8), calls=%async_computation.1 | async-start | bytes 10485760 | tf_op jit(solution)/shard_map/all_to_all | solution.py:12
  21.6 98.2 %all-gather.2.cloned.1.call-start = ((), (), s32[]{:S(2)}) async-start(), calls=%async_computation.3 | async-start | bytes 2027520 | tf_op jit(solution)/shard_map/all_gather | solution.py:64
  22.3 271.3 %reduce-scatter.5.cloned.1.call-start = ((), (), s32[]{:S(2)}) async-start(), calls=%async_computation.5 | async-start | bytes 2027520 | tf_op jit(solution)/shard_map/reduce_scatter | solution.py:79
  22.4 34.0 %collective-permute-start = (bf16[3,512,320]{1,2,0:T(8,128)(2,1)S(1)}, bf16[3,512,320]{1,2,0:T(8,128)(2,1)S(1)}, u32[]{:S(2)}, u32[]{:S(2)}) collective-permute-start(bf16[3,512,320]{1,2,0:T(8,128)(2,1)S(1)} %copy-done.6), channel_id=1, source_target_pairs={{0,128},{8,136},{16,144},{24,152},{32,160},{40,168},{48,176},{56,1... | collective-permute-start | bytes 2949128 | tf_op jit(solution)/shard_map/ppermute | solution.py:18
  30.7 25.4 %collective-permute-start.1 = (s32[2]{0:T(128)S(1)}, s32[2]{0:T(128)S(1)}, u32[]{:S(2)}, u32[]{:S(2)}) collective-permute-start(s32[2]{0:T(128)S(1)} %pad_add_fusion), channel_id=1, source_target_pairs={{0,128},{8,136},{16,144},{24,152},{32,160},{40,168},{48,176},{56,1... | collective-permute-start | bytes 32 | tf_op jit(solution)/shard_map/ppermute | solution.py:18
  56.5 2.6 copy-start.2
  56.5 2.6 copy-start.4
  59.1 4.0 copy-start
  125.9 24.0 %slice-start.6 = ((s8[5242880]{0:T(1024)(128)(4,1)}), s8[1048576]{0:T(1024)(128)(4,1)S(1)}, s32[]{:S(2)}) async-start(s8[5242880]{0:T(1024)(128)(4,1)} %bitcast.83), calls=%async_computation.12 | async-start | bytes 2097152
  128.4 10.9 %slice-start = ((s8[10485760]{0:T(1024)(128)(4,1)}), s8[4194304]{0:T(1024)(128)(4,1)S(1)}, s32[]{:S(2)}) async-start(s8[10485760]{0:T(1024)(128)(4,1)} %bitcast.78), calls=%async_computation.6 | async-start | bytes 8388608
  128.4 10.9 %slice-start.1 = ((s8[10485760]{0:T(1024)(128)(4,1)}), s8[4194304]{0:T(1024)(128)(4,1)S(1)}, s32[]{:S(2)}) async-start(s8[10485760]{0:T(1024)(128)(4,1)} %bitcast.78), calls=%async_computation.7 | async-start | bytes 8388608
  128.4 10.9 %slice-start.2 = ((s8[10485760]{0:T(1024)(128)(4,1)}), s8[2097152]{0:T(1024)(128)(4,1)S(1)}, s32[]{:S(2)}) async-start(s8[10485760]{0:T(1024)(128)(4,1)} %bitcast.78), calls=%async_computation.8 | async-start | bytes 4194304
  128.4 21.5 %slice-start.7 = ((s8[5242880]{0:T(1024)(128)(4,1)}), s8[4194304]{0:T(1024)(128)(4,1)S(1)}, s32[]{:S(2)}) async-start(s8[5242880]{0:T(1024)(128)(4,1)} %bitcast.83), calls=%async_computation.13 | async-start | bytes 8388608
  145.9 2.2 copy-start.1
  154.0 240.0 %reduce-scatter.3.cloned.1.call-start = ((), (), s32[]{:S(2)}) async-start(), calls=%async_computation.4 | async-start | bytes 5898240 | tf_op jit(solution)/shard_map/reduce_scatter | solution.py:66
  160.2 4.4 %copy-start.5 = (bf16[1,2,512,320]{2,3,0,1:T(8,128)(2,1)S(1)}, bf16[1,2,512,320]{2,3,0,1:T(8,128)(2,1)}, u32[]{:S(2)}) copy-start(bf16[1,2,512,320]{2,3,0,1:T(8,128)(2,1)} %copy-done.4) | copy-start | bytes 1966084
  160.3 11.6 %slice-start.3 = ((s8[10485760]{0:T(1024)(128)(4,1)}), s8[4194304]{0:T(1024)(128)(4,1)S(1)}, s32[]{:S(2)}) async-start(s8[10485760]{0:T(1024)(128)(4,1)} %bitcast.80), calls=%async_computation.9 | async-start | bytes 8388608
  164.6 7.2 %slice-start.4 = ((s8[10485760]{0:T(1024)(128)(4,1)}), s8[4194304]{0:T(1024)(128)(4,1)S(1)}, s32[]{:S(2)}) async-start(s8[10485760]{0:T(1024)(128)(4,1)} %bitcast.80), calls=%async_computation.10 | async-start | bytes 8388608
  164.6 7.2 %slice-start.5 = ((s8[10485760]{0:T(1024)(128)(4,1)}), s8[2097152]{0:T(1024)(128)(4,1)S(1)}, s32[]{:S(2)}) async-start(s8[10485760]{0:T(1024)(128)(4,1)} %bitcast.80), calls=%async_computation.11 | async-start | bytes 4194304
  164.6 7.2 %copy-start.3 = (bf16[1,2,512,320]{2,3,0,1:T(8,128)(2,1)S(1)}, bf16[1,2,512,320]{2,3,0,1:T(8,128)(2,1)}, u32[]{:S(2)}) copy-start(bf16[1,2,512,320]{2,3,0,1:T(8,128)(2,1)} %copy-done.2) | copy-start | bytes 1966084
  171.9 4.6 %copy-start.7 = (bf16[2,5,512,64]{2,3,1,0:T(8,128)(2,1)S(1)}, bf16[2,5,512,64]{2,3,1,0:T(8,128)(2,1)}, u32[]{:S(2)}) copy-start(bf16[2,5,512,64]{2,3,1,0:T(8,128)(2,1)} %fusion.19) | copy-start | bytes 1966084
  177.7 45.8 %collective-permute-start.2 = (bf16[3,512,320]{1,2,0:T(8,128)(2,1)}, bf16[3,512,320]{1,2,0:T(8,128)(2,1)S(1)}, u32[]{:S(2)}, u32[]{:S(2)}) collective-permute-start(bf16[3,512,320]{1,2,0:T(8,128)(2,1)} %slice_bitcast_fusion.1), channel_id=1, source_target_pairs={{0,128},{8,136},{16,144},{24,152},{32,160},{40,168},{48,176},{56,1... | collective-permute-start | bytes 2949128 | tf_op jit(solution)/shard_map/ppermute | solution.py:18
Sparse Core Ops, SparseCore 0:
  24.2 95.5 all-gather.1
  154.2 139.3 reduce-scatter.4
  297.8 96.1 reduce-scatter.2
